TPU v7x, 512 devices: a whole 4x4x16 slice. The times are simulated.
512 devices in a mesh: cuts: 32 (over z, y_hi), angle: 16 (over y_lo, x, core).
Axes of the slice: x: 4, y: 4 (y_hi: 2, y_lo: 2; y = y_hi * 2 + y_lo), z: 16, core: 2. Of those that a mesh axis runs over, the one named last changes fastest.
Arguments:
- density: bfloat16 [32, 576, 256], P('cuts', 'angle'), may hold values from 0.049804688 to 2
- kernel_blocks: bfloat16 [576, 256, 384], P('cuts'), may hold values from -0.015625 to 0.015625
Outputs:
- sinogram: bfloat16 [32, 576, 384], P('cuts', 'angle')
All inputs are finite; a program needn't handle non-finite values.
Results may differ from a plain program's by a relative error of at most 0.0012.
Values may be sent and summed in bfloat16 or wider, within the bound.
No kernel may reach another device: no remote copies, remote signals or barrier semaphores. Data moves between devices by JAX's collectives and lax.ppermute only.
A program may use at most 64 MiB of HBM per device.

v0:
```python
import jax
import jax.numpy as jnp
from jax import lax
from jax.sharding import PartitionSpec as P


def local(density, kernel_blocks):
    angles_dev = density.shape[1]
    offsets_dev = kernel_blocks.shape[0]
    angle_count = lax.axis_size("angle")
    offset_start = lax.axis_index("cuts") * offsets_dev
    block_steps = offset_start // angles_dev
    remainder = offset_start - block_steps * angles_dev
    gathered = lax.all_gather(density, "cuts", axis=0, tiled=True)
    full_cycle = lax.all_gather(gathered, "angle", axis=1, tiled=True)
    doubled = jnp.concatenate([full_cycle, full_cycle[:, :angles_dev]], axis=1)
    window_start = (lax.axis_index("angle") - block_steps - 1) % angle_count * angles_dev
    window = lax.dynamic_slice_in_dim(doubled, window_start, 2 * angles_dev, 1)

    def shifted_rows(offset_lag):
        return lax.dynamic_slice_in_dim(window, angles_dev - remainder - offset_lag, angles_dev, 1)

    offset_lags = jnp.arange(offsets_dev, dtype=jnp.int32)
    stacked = jax.vmap(shifted_rows)(offset_lags)
    contribution = lax.psum_scatter(
        jnp.einsum("lsvr,lrb->svb", stacked, kernel_blocks, preferred_element_type=jnp.float32),
        "cuts",
        scatter_dimension=0,
        tiled=True,
    )
    return contribution.astype(jnp.bfloat16)


def solution(mesh):
    return jax.shard_map(
        local,
        mesh=mesh,
        in_specs=(P("cuts", "angle", None), P("cuts", None, None)),
        out_specs=P("cuts", "angle", None),
        check_vma=False,
    )
```

profile of v0, /device:TPU:6, one launch (start us, length us, event | category | flops | bytes accessed | tf_op | source)
XLA Modules:
  0.0 747.7 jit_solution(466443494181665318)
XLA Ops:
  6.5 0.0 copy-start
  6.5 0.0 all-gather.2.cloned.1.call-start
  6.5 86.7 %all_gather.6 = bf16[32,36,256]{2,1,0:T(8,128)(2,1)S(1)} all-gather(bf16[1,36,256]{2,1,0:T(8,128)(2,1)} %param.2), channel_id=1, replica_groups=mesh['cuts'=32,'angle'=16] {'cuts'}, dimensions={0}, use_global_device_ids=true | all-gather | bytes 608256 | tf_op jit(solution)/shard_map/all_gather | solution.py:14
  93.3 0.9 copy.5
  94.2 0.0 all-gather.2.cloned.1.call-update
  94.2 0.0 reduce-scatter.4.cloned.1.call-start
  94.3 57.7 %all-gather.2.cloned.1.call-done = bf16[32,576,256]{2,0,1:T(8,128)(2,1)} async-done(((bf16[32,36,256]{2,0,1:T(8,128)(2,1)}), bf16[32,576,256]{2,0,1:T(8,128)(2,1)}) %all-gather.2.cloned.1.call-update) | async-done | bytes 9437200 | tf_op jit(solution)/shard_map/all_gather | solution.py:15
  152.1 1.1 slice.7
  153.2 2.7 fusion.2
  155.9 7.0 gather_fusion
  162.9 0.0 copy-done
  162.9 8.4 %fusion = f32[32,36,384,1]{2,0,1,3:T(8,128)S(1)} fusion(bf16[18,32,36,256]{3,1,2,0:T(8,128)(2,1)} %gather_fusion, bf16[18,256,384]{2,1,0:T(8,128)(2,1)S(1)} %copy-done), kind=kOutput, calls=%fused_computation.3 | convolution fusion | flops 4076863488 | bytes 15925248 | tf_op jit(solution)/shard_map/lsvr,lrb->svb/dot_general | solution.py:26
  171.3 2.3 copy.11
  173.6 0.0 reduce-scatter.4.cloned.1.call-update
  173.6 565.8 %reduce-scatter.4.cloned.1.call-done = f32[1,36,384]{2,1,0:T(8,128)} async-done(((f32[32,36,384]{2,1,0:T(8,128)}), f32[1,36,384]{2,1,0:T(8,128)}) %reduce-scatter.4.cloned.1.call-update) | async-done | bytes 55312
  739.5 1.4 convert_element_type.3
  (1 shorter events, 0.0 us)
Async XLA Ops:
  6.5 156.4 %copy-start = (bf16[18,256,384]{2,1,0:T(8,128)(2,1)S(1)}, bf16[18,256,384]{2,1,0:T(8,128)(2,1)}, u32[]{:S(2)}) copy-start(bf16[18,256,384]{2,1,0:T(8,128)(2,1)} %param.3) | copy-start | bytes 10616836
  6.5 145.5 %all-gather.2.cloned.1.call-start = ((), (), s32[]{:S(2)}) async-start(), calls=%async_computation.1 | async-start | bytes 10027008 | tf_op jit(solution)/shard_map/all_gather | solution.py:15
  94.2 645.2 %reduce-scatter.4.cloned.1.call-start = ((), (), s32[]{:S(2)}) async-start(), calls=%async_computation.2 | async-start | bytes 2027520
Sparse Core Ops, SparseCore 0:
  94.3 57.6 all-gather.1
  173.7 565.6 reduce-scatter.3
where the time goes:
time: 748 us
  waiting for transfers between devices  624 us (83%)
  blocking collectives  86.7 us (12%)
  between operations  13.5 us (2%)
  local copies, waits for them, and re-layouts  11.4 us (2%)
  matrix products  8.36 us (1%)
    unnamed x3, waiting for transfers between devices  566 us
    all_gather x1, blocking collectives, local(): gathered = lax.all_gather(density, 'cuts', axis=0, tiled=True)  86.7 us
    all_gather x1, waiting for transfers between devices, local(): full_cycle = lax.all_gather(gathered, 'angle', axis=1, tiled=True)  57.7 us
  transfers between devices with their start and end apart: 2, of which 2 were waited for; matrix products, arithmetic and copies ran while one was open for 0% of the time, Pallas kernels for 0%

commit v1 on v0

--- a/solution.py
+++ b/solution.py
@@ -11,7 +11,10 @@
     offset_start = lax.axis_index("cuts") * offsets_dev
     block_steps = offset_start // angles_dev
     remainder = offset_start - block_steps * angles_dev
-    gathered = lax.all_gather(density, "cuts", axis=0, tiled=True)
+    supply_all_entries = lambda state: jnp.concatenate(
+        lax.all_to_all(jnp.stack([state] * lax.axis_size("cuts")), "cuts", 0, 0), axis=0
+    )
+    gathered = supply_all_entries(density)
     full_cycle = lax.all_gather(gathered, "angle", axis=1, tiled=True)
     doubled = jnp.concatenate([full_cycle, full_cycle[:, :angles_dev]], axis=1)
     window_start = (lax.axis_index("angle") - block_steps - 1) % angle_count * angles_dev

time: 748 us -> 717 us (0.959)
  blocking collectives: 86.7 us -> 56.3 us
    all_gather x1 -> x0, blocking collectives: 86.7 us -> none  [local(): gathered = lax.all_gather(density, 'cuts', axis=0, tiled=True)]
    all_to_all x0 -> x1, blocking collectives: none -> 56.3 us  [local(): lax.all_to_all(jnp.stack([state] * lax.axis_size('cuts')), 'cuts', 0, 0)]
where the time goes in v1:
time: 717 us
  waiting for transfers between devices  622 us (87%)
  blocking collectives  56.3 us (8%)
  between operations  13.5 us (2%)
  local copies, waits for them, and re-layouts  12.3 us (2%)
  matrix products  8.36 us (1%)
    unnamed x3, waiting for transfers between devices  566 us
    all_to_all x1, blocking collectives, local(): lax.all_to_all(jnp.stack([state] * lax.axis_size('cuts')), 'cuts', 0, 0)  56.3 us
    all_gather x1, waiting for transfers between devices, local(): full_cycle = lax.all_gather(gathered, 'angle', axis=1, tiled=True)  56.2 us
  transfers between devices with their start and end apart: 2, of which 2 were waited for; matrix products, arithmetic and copies ran while one was open for 0% of the time, Pallas kernels for 0%

profile of v1, /device:TPU:6, one launch (start us, length us, event | category | flops | bytes accessed | tf_op | source)
XLA Modules:
  0.0 716.8 jit_solution(5891110818376929066)
XLA Ops:
  6.5 0.0 copy-start
  6.5 0.0 all-gather.3.cloned.1.call-start
  6.5 0.9 stack.2
  7.5 56.3 %all_to_all.5 = bf16[32,1,36,256]{3,2,1,0:T(8,128)(2,1)S(1)} all-to-all(bf16[32,1,36,256]{3,2,1,0:T(8,128)(2,1)S(1)} %stack.2), channel_id=1, replica_groups=mesh['cuts'=32,'angle'=16] {'cuts'}, dimensions={0} | all-to-all | bytes 1179648 | tf_op jit(solution)/shard_map/all_to_all | solution.py:15
  63.8 0.9 copy.4
  64.7 0.0 all-gather.3.cloned.1.call-update
  64.7 0.0 reduce-scatter.4.cloned.1.call-start
  64.8 56.2 %all-gather.3.cloned.1.call-done = bf16[32,1,576,256]{3,0,1,2:T(8,128)(2,1)} async-done(((bf16[32,1,36,256]{3,0,1,2:T(8,128)(2,1)}), bf16[32,1,576,256]{3,0,1,2:T(8,128)(2,1)}) %all-gather.3.cloned.1.call-update) | async-done | bytes 9437200 | tf_op jit(solution)/shard_map/all_gather | solution.py:18
  121.1 1.1 slice.7
  122.2 2.7 fusion.2
  124.9 7.0 gather_fusion
  131.9 0.0 copy-done
  131.9 8.4 %fusion = f32[32,36,384,1]{2,0,1,3:T(8,128)S(1)} fusion(bf16[18,32,36,256]{3,1,2,0:T(8,128)(2,1)} %gather_fusion, bf16[18,256,384]{2,1,0:T(8,128)(2,1)S(1)} %copy-done), kind=kOutput, calls=%fused_computation.3 | convolution fusion | flops 4076863488 | bytes 15925248 | tf_op jit(solution)/shard_map/lsvr,lrb->svb/dot_general | solution.py:29
  140.3 2.3 copy.10
  142.6 0.0 reduce-scatter.4.cloned.1.call-update
  142.6 565.9 %reduce-scatter.4.cloned.1.call-done = f32[1,36,384]{2,1,0:T(8,128)} async-done(((f32[32,36,384]{2,1,0:T(8,128)}), f32[1,36,384]{2,1,0:T(8,128)}) %reduce-scatter.4.cloned.1.call-update) | async-done | bytes 55312
  708.6 1.4 convert_element_type.3
  (1 shorter events, 0.0 us)
Async XLA Ops:
  6.5 125.4 %copy-start = (bf16[18,256,384]{2,1,0:T(8,128)(2,1)S(1)}, bf16[18,256,384]{2,1,0:T(8,128)(2,1)}, u32[]{:S(2)}) copy-start(bf16[18,256,384]{2,1,0:T(8,128)(2,1)} %param.3) | copy-start | bytes 10616836
  6.5 114.5 %all-gather.3.cloned.1.call-start = ((), (), s32[]{:S(2)}) async-start(), calls=%async_computation.2 | async-start | bytes 10027008 | tf_op jit(solution)/shard_map/all_gather | solution.py:18
  64.7 643.8 %reduce-scatter.4.cloned.1.call-start = ((), (), s32[]{:S(2)}) async-start(), calls=%async_computation.3 | async-start | bytes 2027520
Sparse Core Ops, SparseCore 0:
  64.8 56.1 all-gather.2
  142.7 565.7 reduce-scatter.3
